TPU v7x, 128 devices: a whole 4x4x4 slice. The times are simulated.
128 devices in a mesh: grp: 8 (over y, core), dev: 16 (over x, z).
Axes of the slice: x: 4, y: 4, z: 4, core: 2. Of those that a mesh axis runs over, the one named last changes fastest.
Arguments:
- tiles: bfloat16 [65536, 128, 128], P(('grp', 'dev')), may hold values from -0.125 to 0.125
- tile_ray: int32 [65536], P(('grp', 'dev')), may hold values from 0 to 31, as said below
- tile_col: int32 [65536], P(('grp', 'dev')), may hold values from 0 to 23, as said below
- touched: int32 [3072], P(('grp', 'dev')), may hold values from 0 to 8191, as said below
- home: int32 [8192], replicated, may hold values from 0 to 8191, as said below
- sketch: bfloat16 [1048576, 128], P(('grp', 'dev')), may hold values from -6 to 6
Outputs:
- basis: float32 [1048576, 128], P(('grp', 'dev'))
- r_factor: float32 [128, 128], replicated
Inputs may be any that keep to these rules, and one draw needn't show every extreme that they name: `home`: A permutation that maps each region of 1024 consecutive voxel blocks, g * 1024 to (g + 1) * 1024 - 1, onto the same range of positions. The 24 entries of device i along grp+dev are distinct voxel blocks whose positions home[v] lie in the region of its group g = i // 16; at most 3 of them have positions stored on any one device (position // 64), and in every group one device stores 3 of the touched blocks of every device of the group. On each device the pairs (tile_ray, tile_col) are distinct. `tile_col`: indexes the device's own 24 entries of touched.
All inputs are finite; a program needn't handle non-finite values.
Results may differ from a plain program's by a relative error of at most 0.0017.
Values may be sent and summed in bfloat16 or wider, within the bound.
A program may use at most 192 MiB of HBM per device.

v0:
```python
import jax
import jax.numpy as jnp
from jax import lax
from jax.sharding import PartitionSpec as P

CAP = 3
RB_DEV = 32
gram_shift = 0.001


def factor_lower(gram_matrix):
    width = gram_matrix.shape[0]
    indices = jnp.arange(width, dtype=jnp.int32)

    def column_step(column, lower):
        pick = (indices == column).astype(jnp.float32)
        row_part = jnp.dot(pick, lower, precision=lax.Precision.HIGHEST)
        target = jnp.dot(gram_matrix, pick, precision=lax.Precision.HIGHEST)
        rest = target - jnp.dot(lower, row_part, precision=lax.Precision.HIGHEST)
        diagonal = jnp.sqrt(jnp.sum(rest * pick))
        fresh = jnp.where(
            indices > column, rest / diagonal, jnp.where(indices == column, diagonal, 0.0)
        )
        return lower + fresh[:, None] * pick[None, :]

    return lax.fori_loop(0, width, column_step, jnp.zeros((width, width), jnp.float32))


def invert_lower(lower):
    width = lower.shape[0]
    indices = jnp.arange(width, dtype=jnp.int32)

    def row_step(row, inverse):
        pick = (indices == row).astype(jnp.float32)
        row_part = jnp.dot(pick, lower, precision=lax.Precision.HIGHEST)
        diagonal = jnp.sum(row_part * pick)
        fresh = (pick - jnp.dot(row_part, inverse, precision=lax.Precision.HIGHEST)) / diagonal
        return inverse + pick[:, None] * fresh[None, :]

    return lax.fori_loop(0, width, row_step, jnp.zeros((width, width), jnp.float32))


def local(tiles, tile_ray, tile_col, touched, home, sketch):
    group_size = lax.axis_size("dev")
    tile_size = tiles.shape[1]
    width = sketch.shape[1]
    block_count = sketch.shape[0] // tile_size
    ntouch = touched.shape[0]
    slot_count = group_size * CAP
    matches = touched[:, None] == jnp.arange(home.shape[0], dtype=jnp.int32)[None, :]
    stored = jnp.sum(jnp.where(matches, home[None, :], 0), axis=1)
    holder = stored // block_count % group_size
    local_row = stored % block_count
    counter = jnp.arange(ntouch, dtype=jnp.int32)
    earlier = (holder[:, None] == holder[None, :]) & (counter[:, None] > counter[None, :])
    position = holder * CAP + jnp.sum(earlier, axis=1)
    placing = position[:, None] == jnp.arange(slot_count, dtype=jnp.int32)[None, :]
    request = (jnp.sum(jnp.where(placing, local_row[:, None] + 1, 0), axis=0) - 1).reshape(
        group_size, CAP
    )
    incoming = lax.all_to_all(request, "dev", split_axis=0, concat_axis=0, tiled=True)
    region_block = stored % (group_size * block_count)
    wanted = region_block[:, None] * tile_size + jnp.arange(tile_size, dtype=jnp.int32)[None, :]
    blank_rows = jnp.zeros((ntouch, tile_size, width), sketch.dtype)
    shard_rows = lax.all_gather(sketch, "dev", axis=0, tiled=True)
    length = shard_rows.shape[0]
    inside = (wanted >= 0) & (wanted < length)
    picked = jnp.take(shard_rows, jnp.clip(wanted, 0, length - 1).reshape(-1), axis=0).reshape(
        ntouch, tile_size, width
    )
    touched_rows = jnp.where(inside[:, :, None], picked, blank_rows)
    batch_rows = min(128, tiles.shape[0])
    rounds = tiles.shape[0] // batch_rows
    tile_steps = tiles.reshape(rounds, batch_rows, tile_size, tile_size)
    ray_steps = tile_ray.reshape(rounds, batch_rows)
    col_steps = tile_col.reshape(rounds, batch_rows)

    def image_step(running, inputs):
        tile_block, ray_block, col_block = inputs
        gathered = jnp.take(touched_rows, col_block, axis=0)
        product = jnp.einsum(
            "tab,tbk->tak", tile_block, gathered, preferred_element_type=jnp.float32
        )
        return (running.at[ray_block].add(product), None)

    images, _ = lax.scan(
        image_step,
        jnp.zeros((RB_DEV, tile_size, width), jnp.float32),
        (tile_steps, ray_steps, col_steps),
    )
    images = images.astype(jnp.bfloat16)

    def normal_step(running, inputs):
        tile_block, ray_block, col_block = inputs
        gathered = jnp.take(images, ray_block, axis=0)
        product = jnp.einsum(
            "tab,tak->tbk", tile_block, gathered, preferred_element_type=jnp.float32
        )
        return (running.at[col_block].add(product), None)

    partial_value, _ = lax.scan(
        normal_step,
        jnp.zeros((ntouch, tile_size, width), jnp.float32),
        (tile_steps, ray_steps, col_steps),
    )
    slot_of = jnp.sum(
        jnp.where(placing, jnp.arange(slot_count, dtype=jnp.int32)[None, :], 0), axis=1
    )
    outgoing = jnp.zeros((slot_count, tile_size, width), jnp.float32).at[slot_of].set(partial_value)
    arrived = lax.all_to_all(
        outgoing.reshape(group_size, CAP, tile_size, width),
        "dev",
        split_axis=0,
        concat_axis=0,
        tiled=True,
    )
    target = incoming.reshape(-1)
    safe_target = jnp.where(target >= 0, target, block_count)
    normal = (
        jnp.zeros((block_count + 1, tile_size, width), jnp.float32)
        .at[safe_target]
        .add(arrived.reshape(slot_count, tile_size, width))
    )
    normal = normal[:block_count].reshape(block_count * tile_size, width)
    gram_matrix = lax.psum(
        jnp.dot(normal.T, normal, precision=lax.Precision.HIGHEST), ("grp", "dev")
    )
    voxels = normal.shape[0] * lax.axis_size("grp") * group_size
    gram_matrix = gram_matrix / voxels + gram_shift * jnp.eye(width, dtype=jnp.float32)
    lower = factor_lower(gram_matrix)
    r_factor = lower.T
    inverse = invert_lower(lower).T
    basis_out = jnp.dot(normal, inverse, precision=lax.Precision.HIGHEST)
    return (basis_out, r_factor)


def solution(mesh):
    in_specs = (
        P(("grp", "dev"), None, None),
        P(("grp", "dev")),
        P(("grp", "dev")),
        P(("grp", "dev")),
        P(),
        P(("grp", "dev"), None),
    )
    out_specs = (P(("grp", "dev"), None), P())
    return jax.shard_map(local, mesh=mesh, in_specs=in_specs, out_specs=out_specs, check_vma=False)
```

profile of v0, /device:TPU:1, one launch (start us, length us, event | category | flops | bytes accessed | tf_op | source)
XLA Modules:
  0.0 1193.9 jit_solution(2345552403613061761)
XLA Ops:
  7.9 1.0 select_reduce_fusion
  10.0 8.5 all-to-all-start
  18.5 21.4 %copy.22 = bf16[512,128,128]{1,2,0:T(8,128)(2,1)} copy(bf16[512,128,128]{2,1,0:T(8,128)(2,1)} %param.14) | data formatting | bytes 33554432 | tf_op args[0]
  40.1 170.2 %all-gather.2.cloned.1.call-done = bf16[131072,128]{1,0:T(8,128)(2,1)} async-done(((bf16[8192,128]{1,0:T(8,128)(2,1)}), bf16[131072,128]{1,0:T(8,128)(2,1)}) %all-gather.2.cloned.1.call-update) | async-done | bytes 33554448 | tf_op jit(solution)/shard_map/all_gather | solution.py:65
  210.3 32.8 %gather_fusion.2 = bf16[3072,128]{1,0:T(8,128)(2,1)S(1)} fusion(bf16[131072,128]{1,0:T(8,128)(2,1)} %all-gather.2.cloned.1.call-done, s32[3072]{0:T(1024)S(1)} %broadcast_clamp_fusion), kind=kCustom, calls=%fused_computation.2 | custom fusion | bytes 1585152 | tf_op jit(solution)/shard_map/jit(_take)/gather | solution.py:68
  243.1 1.2 select_select_fusion
  244.6 113.0 %while.49 = (s32[]{:T(128)}, f32[32,128,128]{2,1,0:T(8,128)S(1)}, s32[4,128]{1,0:T(4,128)S(1)}, bf16[4,128,128,128]{3,2,1,0:T(8,128)(2,1)}, s32[4,128]{1,0:T(4,1...) while((s32[]{:T(128)}, f32[32,128,128]{2,1,0:T(8,128)S(1)}, s32[4,128]{1,0:T(4,128)S(1)}, ...), condition=%wide.region_6.7_spmd, body=%wide.region_4.6_spmd.sunk | while | flops 541067776 | bytes 50340692 | solution.py:86
  244.6 3.1 gather_fusion
  247.7 8.0 fusion.97
  255.7 17.1 %scatter_fusion = f32[32,128,128]{2,1,0:T(8,128)S(1)} fusion(f32[32,128,128]{2,1,0:T(8,128)S(1)} %get-tuple-element.482, s32[128]{0:T(128)S(1)} %get-tuple-element.454, f32[128,128,128]{2,1,0:T(8,128)} %fusion.97), kind=kCustom, calls=%fused_computation.3.clone.1 | custom fusion | flops 2097152 | bytes 25166336 | tf_op jit(solution)/shard_map/while/body/eval_jaxpr/scatter-add | solution.py:84
  272.8 3.1 gather_fusion
  276.0 8.0 fusion.97
  284.0 17.1 %scatter_fusion = f32[32,128,128]{2,1,0:T(8,128)S(1)} fusion(f32[32,128,128]{2,1,0:T(8,128)S(1)} %get-tuple-element.482, s32[128]{0:T(128)S(1)} %get-tuple-element.454, f32[128,128,128]{2,1,0:T(8,128)} %fusion.97), kind=kCustom, calls=%fused_computation.3.clone.1 | custom fusion | flops 2097152 | bytes 25166336 | tf_op jit(solution)/shard_map/while/body/eval_jaxpr/scatter-add | solution.py:84
  301.1 3.1 gather_fusion
  304.2 8.0 fusion.97
  312.2 17.1 %scatter_fusion = f32[32,128,128]{2,1,0:T(8,128)S(1)} fusion(f32[32,128,128]{2,1,0:T(8,128)S(1)} %get-tuple-element.482, s32[128]{0:T(128)S(1)} %get-tuple-element.454, f32[128,128,128]{2,1,0:T(8,128)} %fusion.97), kind=kCustom, calls=%fused_computation.3.clone.1 | custom fusion | flops 2097152 | bytes 25166336 | tf_op jit(solution)/shard_map/while/body/eval_jaxpr/scatter-add | solution.py:84
  329.3 3.1 gather_fusion
  332.4 8.0 fusion.97
  340.5 17.0 %scatter_fusion = f32[32,128,128]{2,1,0:T(8,128)S(1)} fusion(f32[32,128,128]{2,1,0:T(8,128)S(1)} %get-tuple-element.482, s32[128]{0:T(128)S(1)} %get-tuple-element.454, f32[128,128,128]{2,1,0:T(8,128)} %fusion.97), kind=kCustom, calls=%fused_computation.3.clone.1 | custom fusion | flops 2097152 | bytes 25166336 | tf_op jit(solution)/shard_map/while/body/eval_jaxpr/scatter-add | solution.py:84
  357.9 112.9 %while.50 = (s32[]{:T(128)}, f32[24,128,128]{2,1,0:T(8,128)S(1)}, s32[4,128]{1,0:T(4,128)S(1)}, bf16[4,128,128,128]{2,3,1,0:T(8,128)(2,1)}, s32[4,128]{1,0:T(4,1...) while((s32[]{:T(128)}, f32[24,128,128]{2,1,0:T(8,128)S(1)}, s32[4,128]{1,0:T(4,128)S(1)}, ...), condition=%wide.region_9.10_spmd, body=%wide.region_7.9_spmd.sunk | while | flops 541067776 | bytes 50340692 | solution.py:101
  357.9 3.1 gather_fusion.1
  361.0 8.0 fusion.101
  369.0 17.0 %scatter_fusion.1 = f32[24,128,128]{2,1,0:T(8,128)S(1)} fusion(f32[24,128,128]{2,1,0:T(8,128)S(1)} %get-tuple-element.503, s32[128]{0:T(128)S(1)} %get-tuple-element.462, f32[128,128,128]{2,1,0:T(8,128)} %fusion.101), kind=kCustom, calls=%fused_computation.4.clone.1 | custom fusion | flops 2097152 | bytes 25166336 | tf_op jit(solution)/shard_map/while/body/eval_jaxpr/scatter-add | solution.py:99
  386.1 3.1 gather_fusion.1
  389.2 8.0 fusion.101
  397.3 17.1 %scatter_fusion.1 = f32[24,128,128]{2,1,0:T(8,128)S(1)} fusion(f32[24,128,128]{2,1,0:T(8,128)S(1)} %get-tuple-element.503, s32[128]{0:T(128)S(1)} %get-tuple-element.462, f32[128,128,128]{2,1,0:T(8,128)} %fusion.101), kind=kCustom, calls=%fused_computation.4.clone.1 | custom fusion | flops 2097152 | bytes 25166336 | tf_op jit(solution)/shard_map/while/body/eval_jaxpr/scatter-add | solution.py:99
  414.4 3.1 gather_fusion.1
  417.5 8.0 fusion.101
  425.5 17.0 %scatter_fusion.1 = f32[24,128,128]{2,1,0:T(8,128)S(1)} fusion(f32[24,128,128]{2,1,0:T(8,128)S(1)} %get-tuple-element.503, s32[128]{0:T(128)S(1)} %get-tuple-element.462, f32[128,128,128]{2,1,0:T(8,128)} %fusion.101), kind=kCustom, calls=%fused_computation.4.clone.1 | custom fusion | flops 2097152 | bytes 25166336 | tf_op jit(solution)/shard_map/while/body/eval_jaxpr/scatter-add | solution.py:99
  442.6 3.1 gather_fusion.1
  445.7 8.0 fusion.101
  453.7 17.0 %scatter_fusion.1 = f32[24,128,128]{2,1,0:T(8,128)S(1)} fusion(f32[24,128,128]{2,1,0:T(8,128)S(1)} %get-tuple-element.503, s32[128]{0:T(128)S(1)} %get-tuple-element.462, f32[128,128,128]{2,1,0:T(8,128)} %fusion.101), kind=kCustom, calls=%fused_computation.4.clone.1 | custom fusion | flops 2097152 | bytes 25166336 | tf_op jit(solution)/shard_map/while/body/eval_jaxpr/scatter-add | solution.py:99
  470.8 2.0 broadcast_in_dim.133
  472.8 5.4 scatter_fusion.2
  478.3 4.9 all-to-all-start.1
  484.0 1.4 reduce.3
  485.4 38.4 %all-to-all-done.1 = f32[16,3,128,128]{3,2,1,0:T(8,128)S(1)} async-done(((f32[16,3,128,128]{3,2,1,0:T(8,128)}), f32[16,3,128,128]{3,2,1,0:T(8,128)S(1)}, u32[]{:S(2)}, u32[]{:S(2)}) %all-to-all-start.1) | async-done | bytes 3145760 | tf_op jit(solution)/shard_map/all_to_all | solution.py:110
  523.8 2.5 broadcast_in_dim.127
  526.3 10.1 scatter_fusion.3
  536.4 10.8 convolution_bitcast_fusion.4
  547.3 4.7 slice.10
  551.9 139.6 %all-reduce.2.cloned.1.call-done = f32[128,128]{1,0:T(8,128)} async-done(((f32[128,128]{1,0:T(8,128)}), f32[128,128]{1,0:T(8,128)}) %all-reduce.2.cloned.1.call-update) | async-done | bytes 65552 | tf_op jit(solution)/shard_map/psum | solution.py:125
  692.4 255.7 %while.52 = (s32[]{:T(128)}, f32[128,128]{1,0:T(8,128)S(1)}, f32[128,128]{1,0:T(8,128)S(1)}, s32[]{:T(128)}, s32[]{:T(128)}) while((s32[]{:T(128)}, f32[128,128]{1,0:T(8,128)S(1)}, f32[128,128]{1,0:T(8,128)S(1)}, s32[]{:T(128)}, s32[]{:T(128)}) %tuple.118), condition=%wide.region_15.16_spmd.clone.clone, body=%wide.region_13.15_spmd.clone.clone.sunk | while | flops 673410 | bytes 332909 | solution.py:26
  692.7 0.9 fusion.114
  694.7 0.9 fusion.114
  696.7 0.9 fusion.114
  948.8 231.7 %while.51 = (s32[]{:T(128)}, f32[128,128]{1,0:T(8,128)S(1)}, f32[128,128]{1,0:T(8,128)S(1)}, s32[]{:T(128)}, s32[]{:T(128)}) while((s32[]{:T(128)}, f32[128,128]{1,0:T(8,128)S(1)}, f32[128,128]{1,0:T(8,128)S(1)}, s32[]{:T(128)}, s32[]{:T(128)}) %tuple.121), condition=%wide.region_18.19_spmd.clone, body=%wide.region_16.18_spmd.clone.sunk | while | flops 460034 | bytes 265308 | solution.py:40
  1180.5 6.5 fusion.66
  (1331 shorter events, 392.2 us)
Async XLA Ops:
  7.2 203.1 %all-gather.2.cloned.1.call-start = ((), (), s32[]{:S(2)}) async-start(), calls=%async_computation.2 | async-start | bytes 35651584 | tf_op jit(solution)/shard_map/all_gather | solution.py:65
  10.0 468.3 %all-to-all-start = ((s32[16,1,3]{2,1,0:T(1,128)}), s32[16,1,3]{2,1,0:T(1,128)}, u32[]{:S(2)}, u32[]{:S(2)}) async-start(s32[16,1,3]{2,1,0:T(1,128)} %bitcast.12), calls=%async_computation | async-start | bytes 16384 | tf_op jit(solution)/shard_map/all_to_all | solution.py:61
  40.1 204.4 %copy-start = (s32[512]{0:T(512)S(1)}, s32[512]{0:T(512)}, u32[]{:S(2)}) copy-start(s32[512]{0:T(512)} %param.16) | copy-start | bytes 6148
  40.1 204.4 %copy-start.1 = (s32[512]{0:T(512)S(1)}, s32[512]{0:T(512)}, u32[]{:S(2)}) copy-start(s32[512]{0:T(512)} %param.15) | copy-start | bytes 6148
  478.3 45.5 %all-to-all-start.1 = ((f32[16,3,128,128]{3,2,1,0:T(8,128)}), f32[16,3,128,128]{3,2,1,0:T(8,128)S(1)}, u32[]{:S(2)}, u32[]{:S(2)}) async-start(f32[16,3,128,128]{3,2,1,0:T(8,128)} %bitcast.134), calls=%async_computation.1 | async-start | bytes 6291456 | tf_op jit(solution)/shard_map/all_to_all | solution.py:110
  483.2 208.3 %all-reduce.2.cloned.1.call-start = ((), (), s32[]{:S(2)}) async-start(), calls=%async_computation.3 | async-start | bytes 131072 | tf_op jit(solution)/shard_map/psum | solution.py:125
Sparse Core Ops, SparseCore 0:
  10.1 200.1 all-gather.1
  547.4 144.0 all-reduce.1
where the time goes:
time: 1200 us; the launch traced here: 1190 us
  matrix products  446 us (37%)
  waiting for transfers between devices  349 us (29%)
  other arithmetic  177 us (15%)
  loops' own time  98.1 us (8%)
  local copies, waits for them, and re-layouts  96.1 us (8%)
  between operations  14.2 us (1%)
  starting transfers between devices  13.7 us (1%)
    all_gather x1, waiting for transfers between devices, local(): shard_rows = lax.all_gather(sketch, 'dev', axis=0, tiled=True)  170 us
    psum x1, waiting for transfers between devices, local(): lax.psum(jnp.dot(normal.T, normal, precision=lax.Precision.HIGHEST), ('gr...  140 us
    dot_general x128, matrix products, column_step(): rest = target - jnp.dot(lower, row_part, precision=lax.Precision.HIGHEST)  113 us
    dot_general x128, matrix products, row_step(): jnp.dot(row_part, inverse, precision=lax.Precision.HIGHEST)  108 us
    dot_general x128, matrix products, row_step(): row_part = jnp.dot(pick, lower, precision=lax.Precision.HIGHEST)  107 us
    another operation x1, loops' own time, factor_lower(): lax.fori_loop(0, width, column_step, jnp.zeros((width, width), jnp.float32))  94 us
    scatter-add x4, other arithmetic, image_step(): return (running.at[ray_block].add(product), None)  68.2 us
    scatter-add x4, other arithmetic, normal_step(): return (running.at[col_block].add(product), None)  68.2 us
  transfers between devices with their start and end apart: 4, of which 3 were waited for; matrix products, arithmetic and copies ran while one was open for 25% of the time, Pallas kernels for 0%

commit v1 on v0

--- a/solution.py
+++ b/solution.py
@@ -122,9 +122,9 @@
         .add(arrived.reshape(slot_count, tile_size, width))
     )
     normal = normal[:block_count].reshape(block_count * tile_size, width)
-    gram_matrix = lax.psum(
-        jnp.dot(normal.T, normal, precision=lax.Precision.HIGHEST), ("grp", "dev")
-    )
+    block = jnp.dot(normal.T, normal, precision=lax.Precision.HIGHEST)
+    blocks = lax.all_gather(block, ("grp", "dev"))
+    gram_matrix = jnp.sum(blocks, axis=0)
     voxels = normal.shape[0] * lax.axis_size("grp") * group_size
     gram_matrix = gram_matrix / voxels + gram_shift * jnp.eye(width, dtype=jnp.float32)
     lower = factor_lower(gram_matrix)

time: 1200 us -> 1130 us (0.942)
  waiting for transfers between devices: 349 us -> 279 us
    psum x1 -> x0, waiting for transfers between devices: 140 us -> none  [local(): lax.psum(jnp.dot(normal.T, normal, precision=lax.Precision.HIGHEST), ('gr...]
    all_gather x0 -> x1, waiting for transfers between devices: none -> 69.9 us  [local(): blocks = lax.all_gather(block, ('grp', 'dev'))]
  transfers between devices with their start and end apart: 4 -> 4, of which waited for: 3 -> 3; matrix products, arithmetic and copies ran while one was open for 25% -> 26% of each run, Pallas kernels for 0% -> 0%
where the time goes in v1:
time: 1130 us
  matrix products  446 us (39%)
  waiting for transfers between devices  279 us (25%)
  other arithmetic  180 us (16%)
  loops' own time  98.1 us (9%)
  local copies, waits for them, and re-layouts  96.1 us (9%)
  between operations  14.2 us (1%)
  starting transfers between devices  13.7 us (1%)
    all_gather x1, waiting for transfers between devices, local(): shard_rows = lax.all_gather(sketch, 'dev', axis=0, tiled=True)  170 us
    dot_general x128, matrix products, column_step(): rest = target - jnp.dot(lower, row_part, precision=lax.Precision.HIGHEST)  113 us
    dot_general x128, matrix products, row_step(): jnp.dot(row_part, inverse, precision=lax.Precision.HIGHEST)  108 us
    dot_general x128, matrix products, row_step(): row_part = jnp.dot(pick, lower, precision=lax.Precision.HIGHEST)  107 us
    another operation x1, loops' own time, factor_lower(): lax.fori_loop(0, width, column_step, jnp.zeros((width, width), jnp.float32))  94 us
    all_gather x1, waiting for transfers between devices, local(): blocks = lax.all_gather(block, ('grp', 'dev'))  69.9 us
    scatter-add x4, other arithmetic, image_step(): return (running.at[ray_block].add(product), None)  68.2 us
    scatter-add x4, other arithmetic, normal_step(): return (running.at[col_block].add(product), None)  68.2 us
  transfers between devices with their start and end apart: 4, of which 3 were waited for; matrix products, arithmetic and copies ran while one was open for 26% of the time, Pallas kernels for 0%

profile of v1, /device:TPU:1, one launch (start us, length us, event | category | flops | bytes accessed | tf_op | source)
XLA Modules:
  0.0 1126.4 jit_solution(3198701545785937318)
XLA Ops:
  7.9 1.0 select_reduce_fusion
  10.0 8.5 all-to-all-start
  18.5 21.4 %copy.22 = bf16[512,128,128]{1,2,0:T(8,128)(2,1)} copy(bf16[512,128,128]{2,1,0:T(8,128)(2,1)} %param.14) | data formatting | bytes 33554432 | tf_op args[0]
  40.1 170.2 %all-gather.4.cloned.1.call-done = bf16[131072,128]{1,0:T(8,128)(2,1)} async-done(((bf16[8192,128]{1,0:T(8,128)(2,1)}), bf16[131072,128]{1,0:T(8,128)(2,1)}) %all-gather.4.cloned.1.call-update) | async-done | bytes 33554448 | tf_op jit(solution)/shard_map/all_gather | solution.py:65
  210.3 32.8 %gather_fusion.2 = bf16[3072,128]{1,0:T(8,128)(2,1)S(1)} fusion(bf16[131072,128]{1,0:T(8,128)(2,1)} %all-gather.4.cloned.1.call-done, s32[3072]{0:T(1024)S(1)} %broadcast_clamp_fusion), kind=kCustom, calls=%fused_computation.2 | custom fusion | bytes 1585152 | tf_op jit(solution)/shard_map/jit(_take)/gather | solution.py:68
  243.1 1.2 select_select_fusion
  244.6 113.0 %while.49 = (s32[]{:T(128)}, f32[32,128,128]{2,1,0:T(8,128)S(1)}, s32[4,128]{1,0:T(4,128)S(1)}, bf16[4,128,128,128]{3,2,1,0:T(8,128)(2,1)}, s32[4,128]{1,0:T(4,1...) while((s32[]{:T(128)}, f32[32,128,128]{2,1,0:T(8,128)S(1)}, s32[4,128]{1,0:T(4,128)S(1)}, ...), condition=%wide.region_6.7_spmd, body=%wide.region_4.6_spmd.sunk | while | flops 541067776 | bytes 50340692 | solution.py:86
  244.6 3.1 gather_fusion
  247.7 8.0 fusion.97
  255.7 17.1 %scatter_fusion = f32[32,128,128]{2,1,0:T(8,128)S(1)} fusion(f32[32,128,128]{2,1,0:T(8,128)S(1)} %get-tuple-element.482, s32[128]{0:T(128)S(1)} %get-tuple-element.454, f32[128,128,128]{2,1,0:T(8,128)} %fusion.97), kind=kCustom, calls=%fused_computation.3.clone.1 | custom fusion | flops 2097152 | bytes 25166336 | tf_op jit(solution)/shard_map/while/body/eval_jaxpr/scatter-add | solution.py:84
  272.8 3.1 gather_fusion
  276.0 8.0 fusion.97
  284.0 17.1 %scatter_fusion = f32[32,128,128]{2,1,0:T(8,128)S(1)} fusion(f32[32,128,128]{2,1,0:T(8,128)S(1)} %get-tuple-element.482, s32[128]{0:T(128)S(1)} %get-tuple-element.454, f32[128,128,128]{2,1,0:T(8,128)} %fusion.97), kind=kCustom, calls=%fused_computation.3.clone.1 | custom fusion | flops 2097152 | bytes 25166336 | tf_op jit(solution)/shard_map/while/body/eval_jaxpr/scatter-add | solution.py:84
  301.1 3.1 gather_fusion
  304.2 8.0 fusion.97
  312.2 17.1 %scatter_fusion = f32[32,128,128]{2,1,0:T(8,128)S(1)} fusion(f32[32,128,128]{2,1,0:T(8,128)S(1)} %get-tuple-element.482, s32[128]{0:T(128)S(1)} %get-tuple-element.454, f32[128,128,128]{2,1,0:T(8,128)} %fusion.97), kind=kCustom, calls=%fused_computation.3.clone.1 | custom fusion | flops 2097152 | bytes 25166336 | tf_op jit(solution)/shard_map/while/body/eval_jaxpr/scatter-add | solution.py:84
  329.3 3.1 gather_fusion
  332.4 8.0 fusion.97
  340.5 17.0 %scatter_fusion = f32[32,128,128]{2,1,0:T(8,128)S(1)} fusion(f32[32,128,128]{2,1,0:T(8,128)S(1)} %get-tuple-element.482, s32[128]{0:T(128)S(1)} %get-tuple-element.454, f32[128,128,128]{2,1,0:T(8,128)} %fusion.97), kind=kCustom, calls=%fused_computation.3.clone.1 | custom fusion | flops 2097152 | bytes 25166336 | tf_op jit(solution)/shard_map/while/body/eval_jaxpr/scatter-add | solution.py:84
  357.9 112.9 %while.50 = (s32[]{:T(128)}, f32[24,128,128]{2,1,0:T(8,128)S(1)}, s32[4,128]{1,0:T(4,128)S(1)}, bf16[4,128,128,128]{2,3,1,0:T(8,128)(2,1)}, s32[4,128]{1,0:T(4,1...) while((s32[]{:T(128)}, f32[24,128,128]{2,1,0:T(8,128)S(1)}, s32[4,128]{1,0:T(4,128)S(1)}, ...), condition=%wide.region_9.10_spmd, body=%wide.region_7.9_spmd.sunk | while | flops 541067776 | bytes 50340692 | solution.py:101
  357.9 3.1 gather_fusion.1
  361.0 8.0 fusion.101
  369.0 17.0 %scatter_fusion.1 = f32[24,128,128]{2,1,0:T(8,128)S(1)} fusion(f32[24,128,128]{2,1,0:T(8,128)S(1)} %get-tuple-element.503, s32[128]{0:T(128)S(1)} %get-tuple-element.462, f32[128,128,128]{2,1,0:T(8,128)} %fusion.101), kind=kCustom, calls=%fused_computation.4.clone.1 | custom fusion | flops 2097152 | bytes 25166336 | tf_op jit(solution)/shard_map/while/body/eval_jaxpr/scatter-add | solution.py:99
  386.1 3.1 gather_fusion.1
  389.2 8.0 fusion.101
  397.3 17.1 %scatter_fusion.1 = f32[24,128,128]{2,1,0:T(8,128)S(1)} fusion(f32[24,128,128]{2,1,0:T(8,128)S(1)} %get-tuple-element.503, s32[128]{0:T(128)S(1)} %get-tuple-element.462, f32[128,128,128]{2,1,0:T(8,128)} %fusion.101), kind=kCustom, calls=%fused_computation.4.clone.1 | custom fusion | flops 2097152 | bytes 25166336 | tf_op jit(solution)/shard_map/while/body/eval_jaxpr/scatter-add | solution.py:99
  414.4 3.1 gather_fusion.1
  417.5 8.0 fusion.101
  425.5 17.0 %scatter_fusion.1 = f32[24,128,128]{2,1,0:T(8,128)S(1)} fusion(f32[24,128,128]{2,1,0:T(8,128)S(1)} %get-tuple-element.503, s32[128]{0:T(128)S(1)} %get-tuple-element.462, f32[128,128,128]{2,1,0:T(8,128)} %fusion.101), kind=kCustom, calls=%fused_computation.4.clone.1 | custom fusion | flops 2097152 | bytes 25166336 | tf_op jit(solution)/shard_map/while/body/eval_jaxpr/scatter-add | solution.py:99
  442.6 3.1 gather_fusion.1
  445.7 8.0 fusion.101
  453.7 17.0 %scatter_fusion.1 = f32[24,128,128]{2,1,0:T(8,128)S(1)} fusion(f32[24,128,128]{2,1,0:T(8,128)S(1)} %get-tuple-element.503, s32[128]{0:T(128)S(1)} %get-tuple-element.462, f32[128,128,128]{2,1,0:T(8,128)} %fusion.101), kind=kCustom, calls=%fused_computation.4.clone.1 | custom fusion | flops 2097152 | bytes 25166336 | tf_op jit(solution)/shard_map/while/body/eval_jaxpr/scatter-add | solution.py:99
  470.8 2.0 broadcast_in_dim.133
  472.8 5.4 scatter_fusion.2
  478.3 4.9 all-to-all-start.1
  484.0 1.4 reduce.3
  485.4 38.4 %all-to-all-done.1 = f32[16,3,128,128]{3,2,1,0:T(8,128)S(1)} async-done(((f32[16,3,128,128]{3,2,1,0:T(8,128)}), f32[16,3,128,128]{3,2,1,0:T(8,128)S(1)}, u32[]{:S(2)}, u32[]{:S(2)}) %all-to-all-start.1) | async-done | bytes 3145760 | tf_op jit(solution)/shard_map/all_to_all | solution.py:110
  523.8 2.5 broadcast_in_dim.127
  526.3 9.4 scatter_fusion.3
  535.7 10.8 convolution_bitcast_fusion.4
  546.6 4.6 slice.10
  551.2 69.9 %all-gather.6.cloned.1.call-done = f32[16384,128]{1,0:T(8,128)} async-done(((f32[128,128]{1,0:T(8,128)}), f32[16384,128]{1,0:T(8,128)}) %all-gather.6.cloned.1.call-update) | async-done | bytes 8388624 | tf_op jit(solution)/shard_map/all_gather | solution.py:126
  621.1 3.8 reduce_sum.78
  624.9 255.7 %while.52 = (s32[]{:T(128)}, f32[128,128]{1,0:T(8,128)S(1)}, f32[128,128]{1,0:T(8,128)S(1)}, s32[]{:T(128)}, s32[]{:T(128)}) while((s32[]{:T(128)}, f32[128,128]{1,0:T(8,128)S(1)}, f32[128,128]{1,0:T(8,128)S(1)}, s32[]{:T(128)}, s32[]{:T(128)}) %tuple.118), condition=%wide.region_15.16_spmd.clone.clone, body=%wide.region_13.15_spmd.clone.clone.sunk | while | flops 673410 | bytes 332909 | solution.py:26
  625.2 0.9 fusion.114
  627.2 0.9 fusion.114
  881.4 231.7 %while.51 = (s32[]{:T(128)}, f32[128,128]{1,0:T(8,128)S(1)}, f32[128,128]{1,0:T(8,128)S(1)}, s32[]{:T(128)}, s32[]{:T(128)}) while((s32[]{:T(128)}, f32[128,128]{1,0:T(8,128)S(1)}, f32[128,128]{1,0:T(8,128)S(1)}, s32[]{:T(128)}, s32[]{:T(128)}) %tuple.121), condition=%wide.region_18.19_spmd.clone, body=%wide.region_16.18_spmd.clone.sunk | while | flops 460034 | bytes 265308 | solution.py:40
  1113.0 6.5 fusion.66
  (1332 shorter events, 392.2 us)
Async XLA Ops:
  7.2 203.1 %all-gather.4.cloned.1.call-start = ((), (), s32[]{:S(2)}) async-start(), calls=%async_computation.2 | async-start | bytes 35651584 | tf_op jit(solution)/shard_map/all_gather | solution.py:65
  10.0 468.3 %all-to-all-start = ((s32[16,1,3]{2,1,0:T(1,128)}), s32[16,1,3]{2,1,0:T(1,128)}, u32[]{:S(2)}, u32[]{:S(2)}) async-start(s32[16,1,3]{2,1,0:T(1,128)} %bitcast.12), calls=%async_computation | async-start | bytes 16384 | tf_op jit(solution)/shard_map/all_to_all | solution.py:61
  40.1 204.4 %copy-start = (s32[512]{0:T(512)S(1)}, s32[512]{0:T(512)}, u32[]{:S(2)}) copy-start(s32[512]{0:T(512)} %param.16) | copy-start | bytes 6148
  40.1 204.4 %copy-start.1 = (s32[512]{0:T(512)S(1)}, s32[512]{0:T(512)}, u32[]{:S(2)}) copy-start(s32[512]{0:T(512)} %param.15) | copy-start | bytes 6148
  478.3 45.5 %all-to-all-start.1 = ((f32[16,3,128,128]{3,2,1,0:T(8,128)}), f32[16,3,128,128]{3,2,1,0:T(8,128)S(1)}, u32[]{:S(2)}, u32[]{:S(2)}) async-start(f32[16,3,128,128]{3,2,1,0:T(8,128)} %bitcast.135), calls=%async_computation.1 | async-start | bytes 6291456 | tf_op jit(solution)/shard_map/all_to_all | solution.py:110
  483.2 137.9 %all-gather.6.cloned.1.call-start = ((), (), s32[]{:S(2)}) async-start(), calls=%async_computation.3 | async-start | bytes 8454144 | tf_op jit(solution)/shard_map/all_gather | solution.py:126
Sparse Core Ops, SparseCore 0:
  10.1 200.1 all-gather.3
  546.7 74.3 all-gather.5
